TPU v7x, 32 devices: a whole 2x2x4 slice. The times are simulated.
32 devices in a mesh: row: 4 (over z), col: 8 (over y, x, core).
Axes of the slice: x: 2, y: 2, z: 4, core: 2. Of those that a mesh axis runs over, the one named last changes fastest.
Arguments:
- solution: float32 [8, 8, 4, 8, 256], P(None, None, 'row', 'col'), may hold values from -6 to 6
- residual: float32 [8, 8, 4, 8, 256], P(None, None, 'row', 'col'), may hold values from -120 to 120
- direction: float32 [8, 8, 4, 8, 256], P(None, None, 'row', 'col'), may hold values from -120 to 120
- noise_var: float32 [8, 4, 8, 256], P(None, 'row', 'col'), may hold values from 2 to 4
- coords: float32 [3, 8, 4, 8, 256], P(None, None, 'row', 'col'), may hold values from 0 to 128
- tile_pairs: int32 [2, 4, 8, 64], P(None, 'row', 'col'), may hold values from 0 to 63, as said below
- tile_count: int32 [4, 8], P('row', 'col'), may hold values from 1 to 64, as said below
Outputs:
- new_solution: float32 [8, 8, 4, 8, 256], P(None, None, 'row', 'col')
- new_residual: float32 [8, 8, 4, 8, 256], P(None, None, 'row', 'col')
- new_direction: float32 [8, 8, 4, 8, 256], P(None, None, 'row', 'col')
Inputs may be any that keep to these rules, and one draw needn't show every extreme that they name: `tile_pairs`: entry [0, g, h, s] is one of the 64 row tiles of cell (g, h) and entry [1, g, h, s] one of its 32 column tiles; the first tile_count[g, h] pairs of a cell are distinct, and the mirror pair of each of them is live in the cell that holds it, so the kernel that the lists define is symmetric. `tile_count`: some cell holds exactly 64 live pairs.
All inputs are finite; a program needn't handle non-finite values.
Results may differ from a plain program's by a relative error of at most 0.0003.
Values sent between devices are 32-bit elements; how exact they have to be, the bound alone decides.
No kernel may reach another device: no remote copies, remote signals or barrier semaphores. Data moves between devices by JAX's collectives and lax.ppermute only.
A program may use at most 64 MiB of HBM per device.

v0:
```python
import jax
import jax.numpy as jnp
from jax import lax
from jax.sharding import PartitionSpec as P

EPS = 1e-06
KERNEL_SCALE = 0.125
HIGHEST = lax.Precision.HIGHEST


def wendland(target_pts, source_pts):
    delta_x = target_pts[0][:, None] - source_pts[0][None, :]
    delta_y = target_pts[1][:, None] - source_pts[1][None, :]
    delta_z = target_pts[2][:, None] - source_pts[2][None, :]
    distance = jnp.sqrt(delta_x * delta_x + delta_y * delta_y + delta_z * delta_z)
    reach_left = jnp.maximum(1.0 - distance, 0.0)
    squared = reach_left * reach_left
    return squared * squared * (4.0 * distance + 1.0)


def run_tiles(
    partial_value, start_slot, stop_slot, target_ids, source_ids, target_pts, source_pts, source_dir
):

    def add_tile(pair_slot, totals):
        target = target_ids[pair_slot]
        source = source_ids[pair_slot]
        kernel_block = wendland(
            lax.dynamic_index_in_dim(target_pts, target, 1, False),
            lax.dynamic_index_in_dim(source_pts, source, 1, False),
        )
        values = lax.dynamic_index_in_dim(source_dir, source, 1, False)
        contrib = jnp.dot(
            values, kernel_block.T, precision=HIGHEST, preferred_element_type=jnp.float32
        )
        current = lax.dynamic_index_in_dim(totals, target, 1, True)
        return lax.dynamic_update_index_in_dim(totals, current + contrib[:, None, :], target, 1)

    return lax.fori_loop(start_slot, stop_slot, add_tile, partial_value)


def per_device(solution, residual, direction, noise_var, coords, tile_pairs, tile_count):
    side_count, owned_tiles, _, _, tile_size = direction.shape
    pair_count = tile_count.reshape(())
    row_ids = tile_pairs[0].reshape(-1)
    col_ids = tile_pairs[1].reshape(-1)
    squares_now = jnp.sum(residual * residual, axis=(1, 2, 3, 4))
    norm_now = lax.psum(squares_now, ("row", "col"))
    row_pts = lax.all_gather(coords, "col", axis=3, tiled=True).reshape(3, -1, tile_size)
    col_pts, col_dir = (
        lax.all_gather(coords, "row", axis=2, tiled=True),
        lax.all_gather(direction, "row", axis=2, tiled=True),
    )
    col_pts = col_pts.reshape(3, -1, tile_size)
    col_dir = col_dir.reshape(side_count, -1, tile_size)
    partial_value = jnp.zeros((side_count, row_pts.shape[1], tile_size), jnp.float32)
    partial_value = run_tiles(
        partial_value, jnp.int32(0), pair_count, row_ids, col_ids, row_pts, col_pts, col_dir
    )
    folded = lax.psum_scatter(
        partial_value.reshape(side_count, owned_tiles, 1, -1, tile_size),
        "col",
        scatter_dimension=3,
        tiled=True,
    )
    applied = noise_var[None] * direction + KERNEL_SCALE * folded
    curvature = lax.psum(jnp.sum(direction * applied, axis=(1, 2, 3, 4)), ("row", "col"))
    step_size = (norm_now / curvature)[:, None, None, None, None]
    new_solution = solution + step_size * direction
    new_residual = residual - step_size * applied
    norm_next = lax.psum(jnp.sum(new_residual * new_residual, axis=(1, 2, 3, 4)), ("row", "col"))
    beta_ratio = (norm_next / (norm_now + EPS))[:, None, None, None, None]
    new_direction = new_residual + beta_ratio * direction
    return (new_solution, new_residual, new_direction)


def solution(mesh):
    in_specs = (
        P(None, None, "row", "col", None),
        P(None, None, "row", "col", None),
        P(None, None, "row", "col", None),
        P(None, "row", "col", None),
        P(None, None, "row", "col", None),
        P(None, "row", "col", None),
        P("row", "col"),
    )
    out_specs = (
        P(None, None, "row", "col", None),
        P(None, None, "row", "col", None),
        P(None, None, "row", "col", None),
    )
    return jax.shard_map(
        per_device, mesh=mesh, in_specs=in_specs, out_specs=out_specs, check_vma=False
    )
```

profile of v0, /device:TPU:0, one launch (start us, length us, event | category | flops | bytes accessed | tf_op | source)
XLA Modules:
  0.0 572.5 jit_solution(3877492613163081918)
XLA Ops:
  7.2 0.8 copy.22
  8.0 13.9 %all_gather.11 = f32[3,8,4,1,256]{4,3,2,1,0:T(1,128)S(1)} all-gather(f32[3,8,1,1,256]{4,3,2,1,0:T(1,128)S(1)} %copy-done.3), channel_id=1, replica_groups=mesh['row'=4,'col'=8] {'row'}, dimensions={2}, use_global_device_ids=true | all-gather | bytes 122880 | tf_op jit(solution)/shard_map/all_gather | solution.py:51
  21.9 9.8 %all_gather.9 = f32[8,8,4,1,256]{4,3,2,1,0:T(1,128)S(1)} all-gather(f32[8,8,1,1,256]{4,3,2,1,0:T(1,128)S(1)} %copy-done), channel_id=1, replica_groups=mesh['row'=4,'col'=8] {'row'}, dimensions={2}, use_global_device_ids=true | all-gather | bytes 327680 | tf_op jit(solution)/shard_map/all_gather | solution.py:52
  31.7 0.7 reduce
  32.5 9.3 %all_gather.10 = f32[3,8,1,8,256]{4,1,2,0,3:T(8,128)S(1)} all-gather(f32[3,8,1,1,256]{4,1,2,0,3:T(8,128)S(1)} %copy.22), channel_id=1, replica_groups=mesh['row'=4,'col'=8] {'col'}, dimensions={3}, use_global_device_ids=true | all-gather | bytes 221184 | tf_op jit(solution)/shard_map/all_gather | solution.py:49
  42.2 127.4 %while.10 = (s32[]{:T(128)}, f32[8,64,256]{2,0,1:T(8,128)S(1)}, s32[]{:T(128)}, s32[64]{0:T(128)S(1)}, s32[64]{0:T(128)S(1)}, /*index=5*/f32[8,32,256]{2,1,0:T(8...) while((s32[]{:T(128)}, f32[8,64,256]{2,0,1:T(8,128)S(1)}, ...), condition=%wide.region_3.4_spmd, body=%wide.region_2.3_spmd.sunk | while | flops 7276557 | bytes 59699 | solution.py:39
  42.9 0.6 dynamic_slice.31
  45.4 0.6 dynamic_slice.30
  49.2 0.6 dynamic_slice.31
  51.8 0.6 dynamic_slice.30
  55.6 0.6 dynamic_slice.31
  58.1 0.6 dynamic_slice.30
  61.9 0.6 dynamic_slice.31
  64.5 0.6 dynamic_slice.30
  68.3 0.6 dynamic_slice.31
  70.8 0.6 dynamic_slice.30
  74.6 0.6 dynamic_slice.31
  77.1 0.6 dynamic_slice.30
  80.9 0.6 dynamic_slice.31
  83.5 0.6 dynamic_slice.30
  87.3 0.6 dynamic_slice.31
  89.8 0.6 dynamic_slice.30
  93.6 0.6 dynamic_slice.31
  96.2 0.6 dynamic_slice.30
  100.0 0.6 dynamic_slice.31
  102.5 0.6 dynamic_slice.30
  106.3 0.6 dynamic_slice.31
  108.8 0.6 dynamic_slice.30
  115.2 0.6 dynamic_slice.30
  121.5 0.6 dynamic_slice.30
  127.9 0.6 dynamic_slice.30
  131.7 0.6 dynamic_slice.31
  134.2 0.6 dynamic_slice.30
  140.5 0.6 dynamic_slice.30
  146.9 0.6 dynamic_slice.30
  150.7 0.6 dynamic_slice.31
  153.2 0.6 dynamic_slice.30
  159.5 0.6 dynamic_slice.30
  165.9 0.6 dynamic_slice.30
  169.7 1.1 copy.25
  170.8 0.7 copy-done.5
  171.8 310.1 %reduce-scatter.2.cloned.1.call-done = f32[8,8,1,1,256]{4,1,2,0,3:T(8,128)} async-done(((f32[8,8,1,8,256]{4,1,2,0,3:T(8,128)}), f32[8,8,1,1,256]{4,1,2,0,3:T(8,128)}) %reduce-scatter.2.cloned.1.call-update) | async-done | bytes 65552 | tf_op jit(solution)/shard_map/reduce_scatter | solution.py:60
  481.9 1.1 multiply_reduce_fusion.1
  482.9 39.4 %all-reduce = (f32[8]{0:T(128)S(1)}, f32[8]{0:T(128)S(1)}) all-reduce(f32[8]{0:T(128)S(1)} %multiply_reduce_fusion.2, f32[8]{0:T(128)S(1)} %multiply_reduce_fusion.1), channel_id=1, replica_groups=mesh['row'=4,'col'=8] {'row','col'}, use_global_device_ids=true, to_apply=%region_1.0 | all-reduce | flops 16 | bytes 128 | tf_op jit(solution)/shard_map/psum | solution.py:48
  522.5 41.0 %psum.23 = f32[8]{0:T(128)S(1)} all-reduce(f32[8]{0:T(128)S(1)} %get-tuple-element.71), channel_id=1, replica_groups=mesh['row'=4,'col'=8] {'row','col'}, use_global_device_ids=true, to_apply=%region_8.9 | all-reduce | flops 8 | bytes 64 | tf_op jit(solution)/shard_map/psum | solution.py:71
  563.5 0.7 copy.32
  564.3 0.7 copy.33
  565.0 0.7 copy.31
  (94 shorter events, 15.8 us)
Async XLA Ops:
  7.2 0.8 copy-start.3
  7.2 474.7 %reduce-scatter.2.cloned.1.call-start = ((), (), s32[]{:S(2)}) async-start(), calls=%async_computation.1 | async-start | bytes 589824 | tf_op jit(solution)/shard_map/reduce_scatter | solution.py:60
  8.0 13.9 %copy-start.6 = (s32[2,1,1,64]{3,2,1,0:T(1,128)S(1)}, s32[2,1,1,64]{3,2,1,0:T(1,128)}, u32[]{:S(2)}) copy-start(s32[2,1,1,64]{3,2,1,0:T(1,128)} %param.14) | copy-start | bytes 1540
  8.0 13.9 %copy-start = (f32[8,8,1,1,256]{4,3,2,1,0:T(1,128)S(1)}, f32[8,8,1,1,256]{4,3,2,1,0:T(1,128)}, u32[]{:S(2)}) copy-start(f32[8,8,1,1,256]{4,3,2,1,0:T(1,128)} %param.11) | copy-start | bytes 196612
  170.8 0.7 copy-start.5
  170.8 0.9 copy-start.1
  481.9 40.4 %copy-start.2 = (f32[8,8,1,1,256]{4,1,2,0,3:T(8,128)S(1)}, f32[8,8,1,1,256]{4,1,2,0,3:T(8,128)}, u32[]{:S(2)}) copy-start(f32[8,8,1,1,256]{4,1,2,0,3:T(8,128)} %reduce-scatter.2.cloned.1.call-done) | copy-start | bytes 196612
  481.9 40.4 %copy-start.4 = (f32[8,8,1,1,256]{4,3,2,1,0:T(1,128)S(1)}, f32[8,8,1,1,256]{4,3,2,1,0:T(1,128)}, u32[]{:S(2)}) copy-start(f32[8,8,1,1,256]{4,3,2,1,0:T(1,128)} %param.9) | copy-start | bytes 196612
Sparse Core Ops, SparseCore 0:
  170.9 310.8 reduce-scatter.1
where the time goes:
time: 583 us; the launch traced here: 573 us
  waiting for transfers between devices  310 us (53%)
  blocking collectives  113 us (19%)
  loops' own time  93.4 us (16%)
  local copies, waits for them, and re-layouts  29.3 us (5%)
  between operations  14.1 us (2%)
  matrix products  9.73 us (2%)
    reduce_scatter x1, waiting for transfers between devices, per_device(): lax.psum_scatter(partial_value.reshape(side_count, owned_tiles, 1, -1, ti...  310 us
    another operation x1, loops' own time, run_tiles(): return lax.fori_loop(start_slot, stop_slot, add_tile, partial_value)  93.4 us
    psum x1, blocking collectives, per_device(): lax.psum(jnp.sum(new_residual * new_residual, axis=(1, 2, 3, 4)), ('row',...  41 us
    psum x1, blocking collectives, per_device(): norm_now = lax.psum(squares_now, ('row', 'col'))  39.4 us
    all_gather x1, blocking collectives, per_device(): lax.all_gather(coords, 'row', axis=2, tiled=True)  13.9 us
    dynamic_slice x20, local copies, waits for them, and re-layouts, add_tile(): target = target_ids[pair_slot]  11.8 us
    dynamic_slice x20, local copies, waits for them, and re-layouts, add_tile(): source = source_ids[pair_slot]  11.7 us
  transfers between devices with their start and end apart: 1, of which 1 were waited for; matrix products, arithmetic and copies ran while one was open for 0% of the time, Pallas kernels for 0%

commit v1 on v0

--- a/solution.py
+++ b/solution.py
@@ -68,7 +68,10 @@
     step_size = (norm_now / curvature)[:, None, None, None, None]
     new_solution = solution + step_size * direction
     new_residual = residual - step_size * applied
-    norm_next = lax.psum(jnp.sum(new_residual * new_residual, axis=(1, 2, 3, 4)), ("row", "col"))
+    norm_next = jnp.sum(
+        lax.all_gather(jnp.sum(new_residual * new_residual, axis=(1, 2, 3, 4)), ("row", "col")),
+        axis=0,
+    )
     beta_ratio = (norm_next / (norm_now + EPS))[:, None, None, None, None]
     new_direction = new_residual + beta_ratio * direction
     return (new_solution, new_residual, new_direction)

time: 583 us -> 583 us (level)
    psum x1 -> x0, blocking collectives: 41 us -> none  [per_device(): lax.psum(jnp.sum(new_residual * new_residual, axis=(1, 2, 3, 4)), ('row',...]
    unnamed x0 -> x1, blocking collectives: none -> 41 us
where the time goes in v1:
time: 583 us; the launch traced here: 573 us
  waiting for transfers between devices  310 us (53%)
  blocking collectives  113 us (19%)
  loops' own time  93.4 us (16%)
  local copies, waits for them, and re-layouts  29.6 us (5%)
  between operations  14.1 us (2%)
  matrix products  9.73 us (2%)
    reduce_scatter x1, waiting for transfers between devices, per_device(): lax.psum_scatter(partial_value.reshape(side_count, owned_tiles, 1, -1, ti...  310 us
    another operation x1, loops' own time, run_tiles(): return lax.fori_loop(start_slot, stop_slot, add_tile, partial_value)  93.4 us
    unnamed x1, blocking collectives  41 us
    psum x1, blocking collectives, per_device(): norm_now = lax.psum(squares_now, ('row', 'col'))  39.4 us
    all_gather x1, blocking collectives, per_device(): lax.all_gather(coords, 'row', axis=2, tiled=True)  13.9 us
    dynamic_slice x20, local copies, waits for them, and re-layouts, add_tile(): target = target_ids[pair_slot]  11.8 us
    dynamic_slice x20, local copies, waits for them, and re-layouts, add_tile(): source = source_ids[pair_slot]  11.7 us
  transfers between devices with their start and end apart: 1, of which 1 were waited for; matrix products, arithmetic and copies ran while one was open for 0% of the time, Pallas kernels for 0%

profile of v1, /device:TPU:0, one launch (start us, length us, event | category | flops | bytes accessed | tf_op | source)
XLA Modules:
  0.0 572.9 jit_solution(3046663883682435765)
XLA Ops:
  7.2 0.8 copy.23
  8.0 13.9 %all_gather.17 = f32[3,8,4,1,256]{4,3,2,1,0:T(1,128)S(1)} all-gather(f32[3,8,1,1,256]{4,3,2,1,0:T(1,128)S(1)} %copy-done.3), channel_id=1, replica_groups=mesh['row'=4,'col'=8] {'row'}, dimensions={2}, use_global_device_ids=true | all-gather | bytes 122880 | tf_op jit(solution)/shard_map/all_gather | solution.py:51
  21.9 9.8 %all_gather.15 = f32[8,8,4,1,256]{4,3,2,1,0:T(1,128)S(1)} all-gather(f32[8,8,1,1,256]{4,3,2,1,0:T(1,128)S(1)} %copy-done), channel_id=1, replica_groups=mesh['row'=4,'col'=8] {'row'}, dimensions={2}, use_global_device_ids=true | all-gather | bytes 327680 | tf_op jit(solution)/shard_map/all_gather | solution.py:52
  31.7 0.7 reduce
  32.5 9.3 %all_gather.16 = f32[3,8,1,8,256]{4,1,2,0,3:T(8,128)S(1)} all-gather(f32[3,8,1,1,256]{4,1,2,0,3:T(8,128)S(1)} %copy.23), channel_id=1, replica_groups=mesh['row'=4,'col'=8] {'col'}, dimensions={3}, use_global_device_ids=true | all-gather | bytes 221184 | tf_op jit(solution)/shard_map/all_gather | solution.py:49
  42.2 127.4 %while.10 = (s32[]{:T(128)}, f32[8,64,256]{2,0,1:T(8,128)S(1)}, s32[]{:T(128)}, s32[64]{0:T(128)S(1)}, s32[64]{0:T(128)S(1)}, /*index=5*/f32[8,32,256]{2,1,0:T(8...) while((s32[]{:T(128)}, f32[8,64,256]{2,0,1:T(8,128)S(1)}, ...), condition=%wide.region_3.4_spmd, body=%wide.region_2.3_spmd.sunk | while | flops 7276557 | bytes 59699 | solution.py:39
  42.9 0.6 dynamic_slice.31
  45.4 0.6 dynamic_slice.30
  49.2 0.6 dynamic_slice.31
  51.8 0.6 dynamic_slice.30
  55.6 0.6 dynamic_slice.31
  58.1 0.6 dynamic_slice.30
  61.9 0.6 dynamic_slice.31
  64.5 0.6 dynamic_slice.30
  68.3 0.6 dynamic_slice.31
  70.8 0.6 dynamic_slice.30
  74.6 0.6 dynamic_slice.31
  77.1 0.6 dynamic_slice.30
  80.9 0.6 dynamic_slice.31
  83.5 0.6 dynamic_slice.30
  87.3 0.6 dynamic_slice.31
  89.8 0.6 dynamic_slice.30
  93.6 0.6 dynamic_slice.31
  96.2 0.6 dynamic_slice.30
  100.0 0.6 dynamic_slice.31
  102.5 0.6 dynamic_slice.30
  106.3 0.6 dynamic_slice.31
  108.8 0.6 dynamic_slice.30
  115.2 0.6 dynamic_slice.30
  121.5 0.6 dynamic_slice.30
  127.9 0.6 dynamic_slice.30
  131.7 0.6 dynamic_slice.31
  134.2 0.6 dynamic_slice.30
  140.5 0.6 dynamic_slice.30
  146.9 0.6 dynamic_slice.30
  150.7 0.6 dynamic_slice.31
  153.2 0.6 dynamic_slice.30
  159.5 0.6 dynamic_slice.30
  165.9 0.6 dynamic_slice.30
  169.7 1.1 copy.26
  170.8 0.7 copy-done.5
  171.8 310.1 %reduce-scatter.2.cloned.1.call-done = f32[8,8,1,1,256]{4,1,2,0,3:T(8,128)} async-done(((f32[8,8,1,8,256]{4,1,2,0,3:T(8,128)}), f32[8,8,1,1,256]{4,1,2,0,3:T(8,128)}) %reduce-scatter.2.cloned.1.call-update) | async-done | bytes 65552 | tf_op jit(solution)/shard_map/reduce_scatter | solution.py:60
  481.9 1.1 multiply_reduce_fusion.1
  482.9 39.4 %all-reduce.1 = (f32[8]{0:T(128)S(1)}, f32[8]{0:T(128)S(1)}) all-reduce(f32[8]{0:T(128)S(1)} %multiply_reduce_fusion.2, f32[8]{0:T(128)S(1)} %multiply_reduce_fusion.1), channel_id=1, replica_groups=mesh['row'=4,'col'=8] {'row','col'}, use_global_device_ids=true, to_apply=%region_1.0 | all-reduce | flops 16 | bytes 128 | tf_op jit(solution)/shard_map/psum | solution.py:48
  522.7 41.0 %all-reduce = f32[256]{0:T(256)S(1)} all-reduce(f32[256]{0:T(256)S(1)} %dynamic-update-slice), channel_id=2, replica_groups=mesh['row'=4,'col'=8] {'row','col'}, use_global_device_ids=true, to_apply=%add | all-reduce | flops 256 | bytes 2048
  563.8 0.7 copy.33
  564.6 0.7 copy.34
  565.3 0.7 copy.32
  (98 shorter events, 16.2 us)
Async XLA Ops:
  7.2 0.8 copy-start.3
  7.2 474.7 %reduce-scatter.2.cloned.1.call-start = ((), (), s32[]{:S(2)}) async-start(), calls=%async_computation.1 | async-start | bytes 589824 | tf_op jit(solution)/shard_map/reduce_scatter | solution.py:60
  8.0 13.9 %copy-start.6 = (s32[2,1,1,64]{3,2,1,0:T(1,128)S(1)}, s32[2,1,1,64]{3,2,1,0:T(1,128)}, u32[]{:S(2)}) copy-start(s32[2,1,1,64]{3,2,1,0:T(1,128)} %param.14) | copy-start | bytes 1540
  8.0 13.9 %copy-start = (f32[8,8,1,1,256]{4,3,2,1,0:T(1,128)S(1)}, f32[8,8,1,1,256]{4,3,2,1,0:T(1,128)}, u32[]{:S(2)}) copy-start(f32[8,8,1,1,256]{4,3,2,1,0:T(1,128)} %param.11) | copy-start | bytes 196612
  170.8 0.7 copy-start.5
  170.8 0.9 copy-start.1
  481.9 40.4 %copy-start.2 = (f32[8,8,1,1,256]{4,1,2,0,3:T(8,128)S(1)}, f32[8,8,1,1,256]{4,1,2,0,3:T(8,128)}, u32[]{:S(2)}) copy-start(f32[8,8,1,1,256]{4,1,2,0,3:T(8,128)} %reduce-scatter.2.cloned.1.call-done) | copy-start | bytes 196612
  481.9 40.4 %copy-start.4 = (f32[8,8,1,1,256]{4,3,2,1,0:T(1,128)S(1)}, f32[8,8,1,1,256]{4,3,2,1,0:T(1,128)}, u32[]{:S(2)}) copy-start(f32[8,8,1,1,256]{4,3,2,1,0:T(1,128)} %param.9) | copy-start | bytes 196612
Sparse Core Ops, SparseCore 0:
  170.9 310.8 reduce-scatter.1

commit v2 on v0

--- a/solution.py
+++ b/solution.py
@@ -68,7 +68,9 @@
     step_size = (norm_now / curvature)[:, None, None, None, None]
     new_solution = solution + step_size * direction
     new_residual = residual - step_size * applied
-    norm_next = lax.psum(jnp.sum(new_residual * new_residual, axis=(1, 2, 3, 4)), ("row", "col"))
+    norm_next = lax.psum(
+        lax.psum(jnp.sum(new_residual * new_residual, axis=(1, 2, 3, 4)), "col"), "row"
+    )
     beta_ratio = (norm_next / (norm_now + EPS))[:, None, None, None, None]
     new_direction = new_residual + beta_ratio * direction
     return (new_solution, new_residual, new_direction)

time: 583 us -> 565 us (0.969)
  blocking collectives: 113 us -> 95.6 us
    psum x1 -> x2, blocking collectives: 41 us -> 23.3 us  [the longest x1 12.7 us: per_device(): lax.psum(jnp.sum(new_residual * new_residual, axis=(1, 2, 3, 4)), 'col')]
where the time goes in v2:
time: 565 us; the launch traced here: 555 us
  waiting for transfers between devices  310 us (55%)
  blocking collectives  95.6 us (17%)
  loops' own time  93.4 us (17%)
  local copies, waits for them, and re-layouts  29.3 us (5%)
  between operations  14.1 us (2%)
  matrix products  9.73 us (2%)
    reduce_scatter x1, waiting for transfers between devices, per_device(): lax.psum_scatter(partial_value.reshape(side_count, owned_tiles, 1, -1, ti...  310 us
    another operation x1, loops' own time, run_tiles(): return lax.fori_loop(start_slot, stop_slot, add_tile, partial_value)  93.4 us
    psum x1, blocking collectives, per_device(): norm_now = lax.psum(squares_now, ('row', 'col'))  39.4 us
    all_gather x1, blocking collectives, per_device(): lax.all_gather(coords, 'row', axis=2, tiled=True)  13.9 us
    psum x1, blocking collectives, per_device(): lax.psum(jnp.sum(new_residual * new_residual, axis=(1, 2, 3, 4)), 'col')  12.7 us
    dynamic_slice x20, local copies, waits for them, and re-layouts, add_tile(): target = target_ids[pair_slot]  11.8 us
    dynamic_slice x20, local copies, waits for them, and re-layouts, add_tile(): source = source_ids[pair_slot]  11.7 us
  transfers between devices with their start and end apart: 1, of which 1 were waited for; matrix products, arithmetic and copies ran while one was open for 0% of the time, Pallas kernels for 0%

profile of v2, /device:TPU:0, one launch (start us, length us, event | category | flops | bytes accessed | tf_op | source)
XLA Modules:
  0.0 554.8 jit_solution(7096577884687991700)
XLA Ops:
  7.2 0.8 copy.22
  8.0 13.9 %all_gather.11 = f32[3,8,4,1,256]{4,3,2,1,0:T(1,128)S(1)} all-gather(f32[3,8,1,1,256]{4,3,2,1,0:T(1,128)S(1)} %copy-done.3), channel_id=1, replica_groups=mesh['row'=4,'col'=8] {'row'}, dimensions={2}, use_global_device_ids=true | all-gather | bytes 122880 | tf_op jit(solution)/shard_map/all_gather | solution.py:51
  21.9 9.8 %all_gather.9 = f32[8,8,4,1,256]{4,3,2,1,0:T(1,128)S(1)} all-gather(f32[8,8,1,1,256]{4,3,2,1,0:T(1,128)S(1)} %copy-done), channel_id=1, replica_groups=mesh['row'=4,'col'=8] {'row'}, dimensions={2}, use_global_device_ids=true | all-gather | bytes 327680 | tf_op jit(solution)/shard_map/all_gather | solution.py:52
  31.7 0.7 reduce
  32.5 9.3 %all_gather.10 = f32[3,8,1,8,256]{4,1,2,0,3:T(8,128)S(1)} all-gather(f32[3,8,1,1,256]{4,1,2,0,3:T(8,128)S(1)} %copy.22), channel_id=1, replica_groups=mesh['row'=4,'col'=8] {'col'}, dimensions={3}, use_global_device_ids=true | all-gather | bytes 221184 | tf_op jit(solution)/shard_map/all_gather | solution.py:49
  42.2 127.4 %while.10 = (s32[]{:T(128)}, f32[8,64,256]{2,0,1:T(8,128)S(1)}, s32[]{:T(128)}, s32[64]{0:T(128)S(1)}, s32[64]{0:T(128)S(1)}, /*index=5*/f32[8,32,256]{2,1,0:T(8...) while((s32[]{:T(128)}, f32[8,64,256]{2,0,1:T(8,128)S(1)}, ...), condition=%wide.region_3.4_spmd, body=%wide.region_2.3_spmd.sunk | while | flops 7276557 | bytes 59699 | solution.py:39
  42.9 0.6 dynamic_slice.31
  45.4 0.6 dynamic_slice.30
  49.2 0.6 dynamic_slice.31
  51.8 0.6 dynamic_slice.30
  55.6 0.6 dynamic_slice.31
  58.1 0.6 dynamic_slice.30
  61.9 0.6 dynamic_slice.31
  64.5 0.6 dynamic_slice.30
  68.3 0.6 dynamic_slice.31
  70.8 0.6 dynamic_slice.30
  74.6 0.6 dynamic_slice.31
  77.1 0.6 dynamic_slice.30
  80.9 0.6 dynamic_slice.31
  83.5 0.6 dynamic_slice.30
  87.3 0.6 dynamic_slice.31
  89.8 0.6 dynamic_slice.30
  93.6 0.6 dynamic_slice.31
  96.2 0.6 dynamic_slice.30
  100.0 0.6 dynamic_slice.31
  102.5 0.6 dynamic_slice.30
  108.8 0.6 dynamic_slice.30
  115.2 0.6 dynamic_slice.30
  121.5 0.6 dynamic_slice.30
  127.9 0.6 dynamic_slice.30
  131.7 0.6 dynamic_slice.31
  134.2 0.6 dynamic_slice.30
  140.5 0.6 dynamic_slice.30
  146.9 0.6 dynamic_slice.30
  150.7 0.6 dynamic_slice.31
  153.2 0.6 dynamic_slice.30
  159.5 0.6 dynamic_slice.30
  165.9 0.6 dynamic_slice.30
  169.7 1.1 copy.25
  170.8 0.7 copy-done.5
  171.8 310.1 %reduce-scatter.2.cloned.1.call-done = f32[8,8,1,1,256]{4,1,2,0,3:T(8,128)} async-done(((f32[8,8,1,8,256]{4,1,2,0,3:T(8,128)}), f32[8,8,1,1,256]{4,1,2,0,3:T(8,128)}) %reduce-scatter.2.cloned.1.call-update) | async-done | bytes 65552 | tf_op jit(solution)/shard_map/reduce_scatter | solution.py:60
  481.9 1.1 multiply_reduce_fusion.1
  482.9 39.4 %all-reduce = (f32[8]{0:T(128)S(1)}, f32[8]{0:T(128)S(1)}) all-reduce(f32[8]{0:T(128)S(1)} %multiply_reduce_fusion.2, f32[8]{0:T(128)S(1)} %multiply_reduce_fusion.1), channel_id=1, replica_groups=mesh['row'=4,'col'=8] {'row','col'}, use_global_device_ids=true, to_apply=%region_1.0 | all-reduce | flops 16 | bytes 128 | tf_op jit(solution)/shard_map/psum | solution.py:48
  522.5 12.7 %psum.30 = f32[8]{0:T(128)S(1)} all-reduce(f32[8]{0:T(128)S(1)} %get-tuple-element.71), channel_id=1, replica_groups=mesh['row'=4,'col'=8] {'col'}, use_global_device_ids=true, to_apply=%region_8.9 | all-reduce | flops 8 | bytes 64 | tf_op jit(solution)/shard_map/psum | solution.py:72
  535.2 10.6 %psum.31 = f32[8]{0:T(128)S(1)} all-reduce(f32[8]{0:T(128)S(1)} %psum.30), channel_id=1, replica_groups=mesh['row'=4,'col'=8] {'row'}, use_global_device_ids=true, to_apply=%region_9.10 | all-reduce | flops 8 | bytes 64 | tf_op jit(solution)/shard_map/psum | solution.py:71
  545.8 0.7 copy.32
  546.5 0.7 copy.33
  547.2 0.7 copy.31
  (95 shorter events, 16.4 us)
Async XLA Ops:
  7.2 0.8 copy-start.3
  7.2 474.7 %reduce-scatter.2.cloned.1.call-start = ((), (), s32[]{:S(2)}) async-start(), calls=%async_computation.1 | async-start | bytes 589824 | tf_op jit(solution)/shard_map/reduce_scatter | solution.py:60
  8.0 13.9 %copy-start.6 = (s32[2,1,1,64]{3,2,1,0:T(1,128)S(1)}, s32[2,1,1,64]{3,2,1,0:T(1,128)}, u32[]{:S(2)}) copy-start(s32[2,1,1,64]{3,2,1,0:T(1,128)} %param.14) | copy-start | bytes 1540
  8.0 13.9 %copy-start = (f32[8,8,1,1,256]{4,3,2,1,0:T(1,128)S(1)}, f32[8,8,1,1,256]{4,3,2,1,0:T(1,128)}, u32[]{:S(2)}) copy-start(f32[8,8,1,1,256]{4,3,2,1,0:T(1,128)} %param.11) | copy-start | bytes 196612
  170.8 0.7 copy-start.5
  170.8 0.9 copy-start.1
  481.9 40.4 %copy-start.2 = (f32[8,8,1,1,256]{4,1,2,0,3:T(8,128)S(1)}, f32[8,8,1,1,256]{4,1,2,0,3:T(8,128)}, u32[]{:S(2)}) copy-start(f32[8,8,1,1,256]{4,1,2,0,3:T(8,128)} %reduce-scatter.2.cloned.1.call-done) | copy-start | bytes 196612
  481.9 40.4 %copy-start.4 = (f32[8,8,1,1,256]{4,3,2,1,0:T(1,128)S(1)}, f32[8,8,1,1,256]{4,3,2,1,0:T(1,128)}, u32[]{:S(2)}) copy-start(f32[8,8,1,1,256]{4,3,2,1,0:T(1,128)} %param.9) | copy-start | bytes 196612
Sparse Core Ops, SparseCore 0:
  170.9 310.8 reduce-scatter.1
